TPU v7x, 256 devices: a whole 4x4x8 slice. The times are simulated.
256 devices in a mesh: frame: 16 (over z_lo, x), strip: 16 (over z_hi, y, core).
Axes of the slice: x: 4, y: 4, z: 8 (z_hi: 2, z_lo: 4; z = z_hi * 4 + z_lo), core: 2. Of those that a mesh axis runs over, the one named last changes fastest.
Arguments:
- movie: bfloat16 [128, 1024, 2048], P('frame', 'strip'), may hold values from -17 to 22, as said below
Outputs:
- lag_maps: float32 [25, 1024, 2048], P(None, 'strip', 'frame')
Inputs may be any that keep to these rules, and one draw needn't show every extreme that they name: Frames of a camera movie.
All inputs are finite; a program needn't handle non-finite values.
Results may differ from a plain program's by a relative error of at most 0.0004.
Values may be sent and summed in bfloat16 or wider, within the bound.
A program may use at most 64 MiB of HBM per device.

v0:
```python
import jax
import jax.numpy as jnp
from jax import lax
from jax.sharding import PartitionSpec as P


def padded_2(value, sides, width):
    for axis, dim in sides:
        peers, length = (lax.axis_size(axis), value.shape[dim])
        up = [(i, (i + 1) % peers) for i in range(peers - 1)]
        down = [(j, i) for i, j in up]
        last = lax.slice_in_dim(value, length - width, length, axis=dim)
        initial = lax.slice_in_dim(value, 0, width, axis=dim)
        before = lax.ppermute(last, axis, up)
        after = lax.ppermute(initial, axis, down)
        value = jnp.concatenate([before, value, after], axis=dim)
    return value


def lag_products(field, rows, columns):
    centre = field[:, 2 : 2 + rows, 2 : 2 + columns]
    products = []
    for row_lag in range(-2, 3):
        for col_lag in range(-2, 3):
            shifted = field[
                :, 2 + row_lag : 2 + row_lag + rows, 2 + col_lag : 2 + col_lag + columns
            ]
            products.append(jnp.sum(centre * shifted, axis=0))
    return jnp.stack(products)


def pad_columns(field):
    return jnp.pad(field, ((0, 0), (0, 0), (2, 2)))


def body(movie):
    frames_here, rows, width = movie.shape
    frame_count = lax.axis_size("frame")
    frames_total = frames_here * frame_count
    padded = padded_2(movie, (("strip", 1),), 2)
    raw_values = padded.astype(jnp.float32)
    pixel_mean = (
        lax.psum(jnp.sum(raw_values, axis=0).astype(jnp.bfloat16), "frame").astype(jnp.float32)
        / frames_total
    )
    fluctuation = pad_columns(raw_values - pixel_mean)
    lag_share = lax.psum_scatter(
        lag_products(fluctuation, rows, width), "frame", scatter_dimension=2, tiled=True
    )
    return lag_share / frames_total


def solution(mesh):
    return jax.shard_map(
        body,
        mesh=mesh,
        in_specs=(P("frame", "strip", None),),
        out_specs=P(None, "strip", "frame"),
        check_vma=False,
    )
```

profile of v0, /device:TPU:1, one launch (start us, length us, event | category | flops | bytes accessed | tf_op | source)
XLA Modules:
  0.0 431.6 jit_solution(7262845705202753640)
XLA Ops:
  6.5 0.0 copy-start.1
  6.5 0.0 all-reduce.3.cloned.1.call-start
  6.5 1.3 fusion.5
  7.8 4.6 %collective-permute-start = (bf16[8,2,2048]{2,1,0:T(2,128)(2,1)S(1)}, bf16[8,2,2048]{2,1,0:T(2,128)(2,1)S(1)}, u32[]{:S(2)}, u32[]{:S(2)}) collective-permute-start(bf16[8,2,2048]{2,1,0:T(2,128)(2,1)S(1)} %get-tuple-element.36), channel_id=1, source_target_pairs={{0,1},{1,2},{2,3},{3,4},{4,5},{5,6},{6,7},{7,8},{8,9},{9,10},{10,1... | collective-permute-start | bytes 196616 | tf_op jit(solution)/shard_map/ppermute | solution.py:14
  12.4 1.9 collective-permute-start.1
  14.3 0.0 collective-permute-done
  14.4 3.6 collective-permute-done.1
  18.0 3.1 fusion.4
  21.2 0.0 all-reduce.3.cloned.1.call-update
  21.2 0.0 reduce-scatter.2.cloned.1.call-start
  21.2 153.5 %all-reduce.3.cloned.1.call-done = bf16[68,2048]{1,0:T(8,128)(2,1)} async-done(((bf16[68,2048]{1,0:T(8,128)(2,1)}), bf16[68,2048]{1,0:T(8,128)(2,1)}) %all-reduce.3.cloned.1.call-update) | async-done | bytes 278544 | tf_op jit(solution)/shard_map/psum | solution.py:43
  174.7 1.0 convert_multiply_fusion
  175.7 0.0 copy-done.1
  175.7 0.9 convert_subtract_fusion
  176.6 0.0 copy-start
  176.6 2.1 copy-done
  178.7 13.1 %multiply_reduce_fusion = (f32[64,2048]{1,0:T(8,128)}, f32[64,2048]{1,0:T(8,128)}, f32[64,2048]{1,0:T(8,128)}, f32[64,2048]{1,0:T(8,128)}, f32[64,2048]{1,0:T(8,...) fusion(f32[8,68,2048]{2,1,0:T(8,128)S(1)} %convert_subtract_fusion), kind=kLoop, calls=%fused_computation.9 | loop fusion | flops 19660800 | bytes 14155776 | tf_op jit(solution)/shard_map/reduce_sum | solution.py:28
  191.8 45.1 %multiply_reduce_fusion.1 = (f32[64,2048]{1,0:T(8,128)S(1)}, f32[64,2048]{1,0:T(8,128)}, f32[64,2048]{1,0:T(8,128)}, f32[64,2048]{1,0:T(8,128)}, f32[64,2048]{1,...) fusion(f32[8,68,2048]{2,1,0:T(8,128)} %copy-done), kind=kLoop, calls=%fused_computation.10 | loop fusion | flops 29491200 | bytes 33554432 | tf_op jit(solution)/shard_map/reduce_sum | solution.py:28
  236.9 0.0 copy-start.15
  236.9 0.0 copy-start.14
  236.9 0.0 copy-start.8
  236.9 0.0 copy-start.11
  236.9 2.0 bitcast_dynamic-update-slice_fusion.24
  238.9 1.9 bitcast_dynamic-update-slice_fusion.23
  240.9 2.0 bitcast_dynamic-update-slice_fusion.22
  242.8 1.9 bitcast_dynamic-update-slice_fusion.21
  244.8 1.9 bitcast_dynamic-update-slice_fusion.20
  246.7 0.0 copy-done.15
  246.7 0.8 bitcast_dynamic-update-slice_fusion.19
  247.6 0.0 copy-done.14
  247.6 0.8 bitcast_dynamic-update-slice_fusion.18
  248.4 0.0 copy-done.8
  248.4 0.8 bitcast_dynamic-update-slice_fusion.17
  249.2 0.0 copy-done.13
  249.2 0.8 bitcast_dynamic-update-slice_fusion.16
  250.1 0.0 copy-done.12
  250.1 0.9 bitcast_dynamic-update-slice_fusion.15
  250.9 0.0 copy-done.11
  250.9 0.8 bitcast_dynamic-update-slice_fusion.14
  251.8 0.0 copy-done.7
  251.8 0.8 bitcast_dynamic-update-slice_fusion.13
  252.6 0.0 copy-done.10
  252.6 0.8 bitcast_dynamic-update-slice_fusion.12
  253.5 0.0 copy-done.6
  253.5 0.9 bitcast_dynamic-update-slice_fusion.11
  254.3 0.0 copy-done.5
  254.3 0.8 bitcast_dynamic-update-slice_fusion.10
  255.2 0.0 copy-done.4
  255.2 0.8 bitcast_dynamic-update-slice_fusion.9
  256.0 0.0 copy-done.3
  256.0 0.9 bitcast_dynamic-update-slice_fusion.8
  256.9 0.0 copy-done.2
  256.9 0.9 bitcast_dynamic-update-slice_fusion.7
  257.8 0.8 bitcast_dynamic-update-slice_fusion.6
  258.6 0.8 bitcast_dynamic-update-slice_fusion.5
  259.5 0.9 bitcast_dynamic-update-slice_fusion.4
  260.3 0.8 bitcast_dynamic-update-slice_fusion.3
  261.2 0.8 bitcast_dynamic-update-slice_fusion.2
  262.0 0.8 bitcast_dynamic-update-slice_fusion.1
  262.9 0.0 copy-done.9
  262.9 0.9 bitcast_dynamic-update-slice_fusion
  263.7 0.0 reduce-scatter.2.cloned.1.call-update
  263.7 158.9 %reduce-scatter.2.cloned.1.call-done = f32[25,64,128]{2,1,0:T(8,128)} async-done(((f32[25,64,2048]{2,1,0:T(8,128)}), f32[25,64,128]{2,1,0:T(8,128)}) %reduce-scatter.2.cloned.1.call-update) | async-done | bytes 819216 | tf_op jit(solution)/shard_map/reduce_scatter | solution.py:47
  422.6 2.1 broadcast_multiply_fusion
  (10 shorter events, 0.0 us)
Async XLA Ops:
  6.5 169.2 %copy-start.1 = (bf16[8,64,2048]{2,1,0:T(8,128)(2,1)S(1)}, bf16[8,64,2048]{2,1,0:T(8,128)(2,1)}, u32[]{:S(2)}) copy-start(bf16[8,64,2048]{2,1,0:T(8,128)(2,1)} %param.1) | copy-start | bytes 6291460
  6.5 168.1 %all-reduce.3.cloned.1.call-start = ((), (), s32[]{:S(2)}) async-start(), calls=%async_computation.1 | async-start | bytes 589824 | tf_op jit(solution)/shard_map/psum | solution.py:43
  7.8 6.5 %collective-permute-start = (bf16[8,2,2048]{2,1,0:T(2,128)(2,1)S(1)}, bf16[8,2,2048]{2,1,0:T(2,128)(2,1)S(1)}, u32[]{:S(2)}, u32[]{:S(2)}) collective-permute-start(bf16[8,2,2048]{2,1,0:T(2,128)(2,1)S(1)} %get-tuple-element.36), channel_id=1, source_target_pairs={{0,1},{1,2},{2,3},{3,4},{4,5},{5,6},{6,7},{7,8},{8,9},{9,10},{10,1... | collective-permute-start | bytes 196616 | tf_op jit(solution)/shard_map/ppermute | solution.py:14
  12.4 5.6 %collective-permute-start.1 = (bf16[8,2,2048]{2,1,0:T(2,128)(2,1)S(1)}, bf16[8,2,2048]{2,1,0:T(2,128)(2,1)S(1)}, u32[]{:S(2)}, u32[]{:S(2)}) collective-permute-start(bf16[8,2,2048]{2,1,0:T(2,128)(2,1)S(1)} %get-tuple-element.37), channel_id=1, source_target_pairs={{1,0},{2,1},{3,2},{4,3},{5,4},{6,5},{7,6},{8,7},{9,8},{10,9},{11,1... | collective-permute-start | bytes 196616 | tf_op jit(solution)/shard_map/ppermute | solution.py:15
  21.2 401.4 %reduce-scatter.2.cloned.1.call-start = ((), (), s32[]{:S(2)}) async-start(), calls=%async_computation.2 | async-start | bytes 13926400 | tf_op jit(solution)/shard_map/reduce_scatter | solution.py:47
  176.6 2.1 copy-start
  236.9 9.8 %copy-start.15 = (f32[64,2048]{1,0:T(8,128)S(1)}, f32[64,2048]{1,0:T(8,128)}, u32[]{:S(2)}) copy-start(f32[64,2048]{1,0:T(8,128)} %get-tuple-element.9) | copy-start | bytes 1572868
  236.9 10.7 %copy-start.14 = (f32[64,2048]{1,0:T(8,128)S(1)}, f32[64,2048]{1,0:T(8,128)}, u32[]{:S(2)}) copy-start(f32[64,2048]{1,0:T(8,128)} %get-tuple-element.10) | copy-start | bytes 1572868
  236.9 11.5 %copy-start.8 = (f32[64,2048]{1,0:T(8,128)S(1)}, f32[64,2048]{1,0:T(8,128)}, u32[]{:S(2)}) copy-start(f32[64,2048]{1,0:T(8,128)} %get-tuple-element.32) | copy-start | bytes 1572868
  236.9 12.4 %copy-start.13 = (f32[64,2048]{1,0:T(8,128)S(1)}, f32[64,2048]{1,0:T(8,128)}, u32[]{:S(2)}) copy-start(f32[64,2048]{1,0:T(8,128)} %get-tuple-element.11) | copy-start | bytes 1572868
  236.9 13.2 %copy-start.12 = (f32[64,2048]{1,0:T(8,128)S(1)}, f32[64,2048]{1,0:T(8,128)}, u32[]{:S(2)}) copy-start(f32[64,2048]{1,0:T(8,128)} %get-tuple-element.12) | copy-start | bytes 1572868
  236.9 14.1 %copy-start.11 = (f32[64,2048]{1,0:T(8,128)S(1)}, f32[64,2048]{1,0:T(8,128)}, u32[]{:S(2)}) copy-start(f32[64,2048]{1,0:T(8,128)} %get-tuple-element.13) | copy-start | bytes 1572868
  238.9 12.9 %copy-start.7 = (f32[64,2048]{1,0:T(8,128)S(1)}, f32[64,2048]{1,0:T(8,128)}, u32[]{:S(2)}) copy-start(f32[64,2048]{1,0:T(8,128)} %get-tuple-element.16) | copy-start | bytes 1572868
  240.9 11.8 %copy-start.10 = (f32[64,2048]{1,0:T(8,128)S(1)}, f32[64,2048]{1,0:T(8,128)}, u32[]{:S(2)}) copy-start(f32[64,2048]{1,0:T(8,128)} %get-tuple-element.14) | copy-start | bytes 1572868
  242.8 10.7 %copy-start.6 = (f32[64,2048]{1,0:T(8,128)S(1)}, f32[64,2048]{1,0:T(8,128)}, u32[]{:S(2)}) copy-start(f32[64,2048]{1,0:T(8,128)} %get-tuple-element.17) | copy-start | bytes 1572868
  244.8 9.6 %copy-start.5 = (f32[64,2048]{1,0:T(8,128)S(1)}, f32[64,2048]{1,0:T(8,128)}, u32[]{:S(2)}) copy-start(f32[64,2048]{1,0:T(8,128)} %get-tuple-element.18) | copy-start | bytes 1572868
  246.7 8.5 %copy-start.4 = (f32[64,2048]{1,0:T(8,128)S(1)}, f32[64,2048]{1,0:T(8,128)}, u32[]{:S(2)}) copy-start(f32[64,2048]{1,0:T(8,128)} %get-tuple-element.19) | copy-start | bytes 1572868
  247.6 8.5 %copy-start.3 = (f32[64,2048]{1,0:T(8,128)S(1)}, f32[64,2048]{1,0:T(8,128)}, u32[]{:S(2)}) copy-start(f32[64,2048]{1,0:T(8,128)} %get-tuple-element.20) | copy-start | bytes 1572868
  248.4 8.5 %copy-start.2 = (f32[64,2048]{1,0:T(8,128)S(1)}, f32[64,2048]{1,0:T(8,128)}, u32[]{:S(2)}) copy-start(f32[64,2048]{1,0:T(8,128)} %get-tuple-element.33) | copy-start | bytes 1572868
  254.3 8.5 %copy-start.9 = (f32[64,2048]{1,0:T(8,128)S(1)}, f32[64,2048]{1,0:T(8,128)}, u32[]{:S(2)}) copy-start(f32[64,2048]{1,0:T(8,128)} %get-tuple-element.5) | copy-start | bytes 1572868
Sparse Core Ops, SparseCore 0:
  21.3 153.3 all-reduce.2
  263.9 158.7 reduce-scatter.1
where the time goes:
time: 432 us
  waiting for transfers between devices  316 us (73%)
  other arithmetic  65.3 us (15%)
  local copies, waits for them, and re-layouts  30.2 us (7%)
  between operations  13.5 us (3%)
  starting transfers between devices  6.55 us (2%)
    reduce_scatter x1, waiting for transfers between devices, body(): lax.psum_scatter(lag_products(fluctuation, rows, width), 'frame', scatter...  159 us
    psum x1, waiting for transfers between devices, body(): lax.psum(jnp.sum(raw_values, axis=0).astype(jnp.bfloat16), 'frame')  153 us
    reduce_sum x2, other arithmetic, lag_products(): products.append(jnp.sum(centre * shifted, axis=0))  58.2 us
    unnamed x56, local copies, waits for them, and re-layouts  28.1 us
  transfers between devices with their start and end apart: 4, of which 3 were waited for; matrix products, arithmetic and copies ran while one was open for 0% of the time, Pallas kernels for 0%

commit v1 on v0

--- a/solution.py
+++ b/solution.py
@@ -40,7 +40,9 @@
     padded = padded_2(movie, (("strip", 1),), 2)
     raw_values = padded.astype(jnp.float32)
     pixel_mean = (
-        lax.psum(jnp.sum(raw_values, axis=0).astype(jnp.bfloat16), "frame").astype(jnp.float32)
+        jnp.sum(
+            jax.lax.all_gather(jnp.sum(raw_values, axis=0).astype(jnp.bfloat16), "frame"), 0
+        ).astype(jnp.float32)
         / frames_total
     )
     fluctuation = pad_columns(raw_values - pixel_mean)

time: 432 us -> 367 us (0.85)
  waiting for transfers between devices: 316 us -> 249 us
    psum x1 -> x0, waiting for transfers between devices: 153 us -> none  [body(): lax.psum(jnp.sum(raw_values, axis=0).astype(jnp.bfloat16), 'frame')]
    all_gather x0 -> x1, waiting for transfers between devices: none -> 87.1 us  [body(): jax.lax.all_gather(jnp.sum(raw_values, axis=0).astype(jnp.bfloat16), 'fra...]
where the time goes in v1:
time: 367 us
  waiting for transfers between devices  249 us (68%)
  other arithmetic  67.6 us (18%)
  local copies, waits for them, and re-layouts  30.2 us (8%)
  between operations  13.5 us (4%)
  starting transfers between devices  6.55 us (2%)
    reduce_scatter x1, waiting for transfers between devices, body(): lax.psum_scatter(lag_products(fluctuation, rows, width), 'frame', scatter...  158 us
    all_gather x1, waiting for transfers between devices, body(): jax.lax.all_gather(jnp.sum(raw_values, axis=0).astype(jnp.bfloat16), 'fra...  87.1 us
    reduce_sum x2, other arithmetic, lag_products(): products.append(jnp.sum(centre * shifted, axis=0))  58.2 us
    unnamed x56, local copies, waits for them, and re-layouts  28.1 us
  transfers between devices with their start and end apart: 4, of which 3 were waited for; matrix products, arithmetic and copies ran while one was open for 0% of the time, Pallas kernels for 0%

profile of v1, /device:TPU:1, one launch (start us, length us, event | category | flops | bytes accessed | tf_op | source)
XLA Modules:
  0.0 367.0 jit_solution(15659195387499518902)
XLA Ops:
  6.5 0.0 copy-start.1
  6.5 0.0 all-gather.4.cloned.1.call-start
  6.5 1.3 fusion.5
  7.8 4.6 %collective-permute-start = (bf16[8,2,2048]{2,1,0:T(2,128)(2,1)S(1)}, bf16[8,2,2048]{2,1,0:T(2,128)(2,1)S(1)}, u32[]{:S(2)}, u32[]{:S(2)}) collective-permute-start(bf16[8,2,2048]{2,1,0:T(2,128)(2,1)S(1)} %get-tuple-element.36), channel_id=1, source_target_pairs={{0,1},{1,2},{2,3},{3,4},{4,5},{5,6},{6,7},{7,8},{8,9},{9,10},{10,1... | collective-permute-start | bytes 196616 | tf_op jit(solution)/shard_map/ppermute | solution.py:14
  12.4 1.9 collective-permute-start.1
  14.3 0.0 collective-permute-done
  14.4 3.6 collective-permute-done.1
  18.0 3.1 fusion.4
  21.2 0.0 all-gather.4.cloned.1.call-update
  21.2 0.0 reduce-scatter.2.cloned.1.call-start
  21.2 87.1 %all-gather.4.cloned.1.call-done = bf16[16,68,2048]{2,1,0:T(8,128)(2,1)} async-done(((bf16[1,68,2048]{2,1,0:T(8,128)(2,1)}), bf16[16,68,2048]{2,1,0:T(8,128)(2,1)}) %all-gather.4.cloned.1.call-update) | async-done | bytes 4456464 | tf_op jit(solution)/shard_map/all_gather | solution.py:44
  108.3 3.3 reduce_sum.250
  111.6 0.0 copy-done.1
  111.6 0.9 convert_subtract_fusion
  112.5 0.0 copy-start
  112.5 2.1 copy-done
  114.6 13.1 %multiply_reduce_fusion = (f32[64,2048]{1,0:T(8,128)}, f32[64,2048]{1,0:T(8,128)}, f32[64,2048]{1,0:T(8,128)}, f32[64,2048]{1,0:T(8,128)}, f32[64,2048]{1,0:T(8,...) fusion(f32[8,68,2048]{2,1,0:T(8,128)S(1)} %convert_subtract_fusion), kind=kLoop, calls=%fused_computation.9 | loop fusion | flops 19660800 | bytes 14155776 | tf_op jit(solution)/shard_map/reduce_sum | solution.py:28
  127.7 45.1 %multiply_reduce_fusion.1 = (f32[64,2048]{1,0:T(8,128)S(1)}, f32[64,2048]{1,0:T(8,128)}, f32[64,2048]{1,0:T(8,128)}, f32[64,2048]{1,0:T(8,128)}, f32[64,2048]{1,...) fusion(f32[8,68,2048]{2,1,0:T(8,128)} %copy-done), kind=kLoop, calls=%fused_computation.10 | loop fusion | flops 29491200 | bytes 33554432 | tf_op jit(solution)/shard_map/reduce_sum | solution.py:28
  172.8 0.0 copy-start.15
  172.8 0.0 copy-start.14
  172.8 0.0 copy-start.8
  172.8 0.0 copy-start.11
  172.8 2.0 bitcast_dynamic-update-slice_fusion.24
  174.9 1.9 bitcast_dynamic-update-slice_fusion.23
  176.8 2.0 bitcast_dynamic-update-slice_fusion.22
  178.8 1.9 bitcast_dynamic-update-slice_fusion.21
  180.7 1.9 bitcast_dynamic-update-slice_fusion.20
  182.6 0.0 copy-done.15
  182.7 0.8 bitcast_dynamic-update-slice_fusion.19
  183.5 0.0 copy-done.14
  183.5 0.8 bitcast_dynamic-update-slice_fusion.18
  184.3 0.0 copy-done.8
  184.3 0.8 bitcast_dynamic-update-slice_fusion.17
  185.2 0.0 copy-done.13
  185.2 0.8 bitcast_dynamic-update-slice_fusion.16
  186.0 0.0 copy-done.12
  186.0 0.9 bitcast_dynamic-update-slice_fusion.15
  186.9 0.0 copy-done.11
  186.9 0.8 bitcast_dynamic-update-slice_fusion.14
  187.7 0.0 copy-done.7
  187.7 0.8 bitcast_dynamic-update-slice_fusion.13
  188.6 0.0 copy-done.10
  188.6 0.8 bitcast_dynamic-update-slice_fusion.12
  189.4 0.0 copy-done.6
  189.4 0.9 bitcast_dynamic-update-slice_fusion.11
  190.3 0.0 copy-done.5
  190.3 0.8 bitcast_dynamic-update-slice_fusion.10
  191.1 0.0 copy-done.4
  191.1 0.8 bitcast_dynamic-update-slice_fusion.9
  192.0 0.0 copy-done.3
  192.0 0.9 bitcast_dynamic-update-slice_fusion.8
  192.8 0.0 copy-done.2
  192.8 0.9 bitcast_dynamic-update-slice_fusion.7
  193.8 0.8 bitcast_dynamic-update-slice_fusion.6
  194.6 0.8 bitcast_dynamic-update-slice_fusion.5
  195.4 0.9 bitcast_dynamic-update-slice_fusion.4
  196.3 0.8 bitcast_dynamic-update-slice_fusion.3
  197.1 0.8 bitcast_dynamic-update-slice_fusion.2
  197.9 0.8 bitcast_dynamic-update-slice_fusion.1
  198.8 0.0 copy-done.9
  198.8 0.9 bitcast_dynamic-update-slice_fusion
  199.7 0.0 reduce-scatter.2.cloned.1.call-update
  199.7 158.4 %reduce-scatter.2.cloned.1.call-done = f32[25,64,128]{2,1,0:T(8,128)} async-done(((f32[25,64,2048]{2,1,0:T(8,128)}), f32[25,64,128]{2,1,0:T(8,128)}) %reduce-scatter.2.cloned.1.call-update) | async-done | bytes 819216 | tf_op jit(solution)/shard_map/reduce_scatter | solution.py:49
  358.1 2.1 broadcast_multiply_fusion
  (11 shorter events, 0.1 us)
Async XLA Ops:
  6.5 105.1 %copy-start.1 = (bf16[8,64,2048]{2,1,0:T(8,128)(2,1)S(1)}, bf16[8,64,2048]{2,1,0:T(8,128)(2,1)}, u32[]{:S(2)}) copy-start(bf16[8,64,2048]{2,1,0:T(8,128)(2,1)} %param.1) | copy-start | bytes 6291460
  6.5 101.7 %all-gather.4.cloned.1.call-start = ((), (), s32[]{:S(2)}) async-start(), calls=%async_computation.2 | async-start | bytes 5013504 | tf_op jit(solution)/shard_map/all_gather | solution.py:44
  7.8 6.5 %collective-permute-start = (bf16[8,2,2048]{2,1,0:T(2,128)(2,1)S(1)}, bf16[8,2,2048]{2,1,0:T(2,128)(2,1)S(1)}, u32[]{:S(2)}, u32[]{:S(2)}) collective-permute-start(bf16[8,2,2048]{2,1,0:T(2,128)(2,1)S(1)} %get-tuple-element.36), channel_id=1, source_target_pairs={{0,1},{1,2},{2,3},{3,4},{4,5},{5,6},{6,7},{7,8},{8,9},{9,10},{10,1... | collective-permute-start | bytes 196616 | tf_op jit(solution)/shard_map/ppermute | solution.py:14
  12.4 5.6 %collective-permute-start.1 = (bf16[8,2,2048]{2,1,0:T(2,128)(2,1)S(1)}, bf16[8,2,2048]{2,1,0:T(2,128)(2,1)S(1)}, u32[]{:S(2)}, u32[]{:S(2)}) collective-permute-start(bf16[8,2,2048]{2,1,0:T(2,128)(2,1)S(1)} %get-tuple-element.37), channel_id=1, source_target_pairs={{1,0},{2,1},{3,2},{4,3},{5,4},{6,5},{7,6},{8,7},{9,8},{10,9},{11,1... | collective-permute-start | bytes 196616 | tf_op jit(solution)/shard_map/ppermute | solution.py:15
  21.2 336.9 %reduce-scatter.2.cloned.1.call-start = ((), (), s32[]{:S(2)}) async-start(), calls=%async_computation.1 | async-start | bytes 13926400 | tf_op jit(solution)/shard_map/reduce_scatter | solution.py:49
  112.5 2.1 copy-start
  172.8 9.8 %copy-start.15 = (f32[64,2048]{1,0:T(8,128)S(1)}, f32[64,2048]{1,0:T(8,128)}, u32[]{:S(2)}) copy-start(f32[64,2048]{1,0:T(8,128)} %get-tuple-element.9) | copy-start | bytes 1572868
  172.8 10.7 %copy-start.14 = (f32[64,2048]{1,0:T(8,128)S(1)}, f32[64,2048]{1,0:T(8,128)}, u32[]{:S(2)}) copy-start(f32[64,2048]{1,0:T(8,128)} %get-tuple-element.10) | copy-start | bytes 1572868
  172.8 11.5 %copy-start.8 = (f32[64,2048]{1,0:T(8,128)S(1)}, f32[64,2048]{1,0:T(8,128)}, u32[]{:S(2)}) copy-start(f32[64,2048]{1,0:T(8,128)} %get-tuple-element.32) | copy-start | bytes 1572868
  172.8 12.4 %copy-start.13 = (f32[64,2048]{1,0:T(8,128)S(1)}, f32[64,2048]{1,0:T(8,128)}, u32[]{:S(2)}) copy-start(f32[64,2048]{1,0:T(8,128)} %get-tuple-element.11) | copy-start | bytes 1572868
  172.8 13.2 %copy-start.12 = (f32[64,2048]{1,0:T(8,128)S(1)}, f32[64,2048]{1,0:T(8,128)}, u32[]{:S(2)}) copy-start(f32[64,2048]{1,0:T(8,128)} %get-tuple-element.12) | copy-start | bytes 1572868
  172.8 14.1 %copy-start.11 = (f32[64,2048]{1,0:T(8,128)S(1)}, f32[64,2048]{1,0:T(8,128)}, u32[]{:S(2)}) copy-start(f32[64,2048]{1,0:T(8,128)} %get-tuple-element.13) | copy-start | bytes 1572868
  174.9 12.9 %copy-start.7 = (f32[64,2048]{1,0:T(8,128)S(1)}, f32[64,2048]{1,0:T(8,128)}, u32[]{:S(2)}) copy-start(f32[64,2048]{1,0:T(8,128)} %get-tuple-element.16) | copy-start | bytes 1572868
  176.8 11.8 %copy-start.10 = (f32[64,2048]{1,0:T(8,128)S(1)}, f32[64,2048]{1,0:T(8,128)}, u32[]{:S(2)}) copy-start(f32[64,2048]{1,0:T(8,128)} %get-tuple-element.14) | copy-start | bytes 1572868
  178.8 10.7 %copy-start.6 = (f32[64,2048]{1,0:T(8,128)S(1)}, f32[64,2048]{1,0:T(8,128)}, u32[]{:S(2)}) copy-start(f32[64,2048]{1,0:T(8,128)} %get-tuple-element.17) | copy-start | bytes 1572868
  180.7 9.6 %copy-start.5 = (f32[64,2048]{1,0:T(8,128)S(1)}, f32[64,2048]{1,0:T(8,128)}, u32[]{:S(2)}) copy-start(f32[64,2048]{1,0:T(8,128)} %get-tuple-element.18) | copy-start | bytes 1572868
  182.6 8.5 %copy-start.4 = (f32[64,2048]{1,0:T(8,128)S(1)}, f32[64,2048]{1,0:T(8,128)}, u32[]{:S(2)}) copy-start(f32[64,2048]{1,0:T(8,128)} %get-tuple-element.19) | copy-start | bytes 1572868
  183.5 8.5 %copy-start.3 = (f32[64,2048]{1,0:T(8,128)S(1)}, f32[64,2048]{1,0:T(8,128)}, u32[]{:S(2)}) copy-start(f32[64,2048]{1,0:T(8,128)} %get-tuple-element.20) | copy-start | bytes 1572868
  184.3 8.5 %copy-start.2 = (f32[64,2048]{1,0:T(8,128)S(1)}, f32[64,2048]{1,0:T(8,128)}, u32[]{:S(2)}) copy-start(f32[64,2048]{1,0:T(8,128)} %get-tuple-element.33) | copy-start | bytes 1572868
  190.3 8.5 %copy-start.9 = (f32[64,2048]{1,0:T(8,128)S(1)}, f32[64,2048]{1,0:T(8,128)}, u32[]{:S(2)}) copy-start(f32[64,2048]{1,0:T(8,128)} %get-tuple-element.5) | copy-start | bytes 1572868
Sparse Core Ops, SparseCore 0:
  21.3 86.9 all-gather.3
  199.8 158.2 reduce-scatter.1
